TPU v7x, 512 devices: a whole 4x4x16 slice. The times are simulated.
512 devices in a mesh: dp: 8 (over z_hi, y), tm: 64 (over z_lo, x, core).
Axes of the slice: x: 4, y: 4, z: 16 (z_hi: 2, z_lo: 8; z = z_hi * 8 + z_lo), core: 2. Of those that a mesh axis runs over, the one named last changes fastest.
Arguments:
- query_proj: bfloat16 [8, 8192, 768], P('dp', 'tm'), may hold values from -240 to 240
- key_proj: bfloat16 [8, 8192, 768], P('dp', 'tm'), may hold values from -6 to 6
- value_proj: bfloat16 [8, 8192, 768], P('dp', 'tm'), may hold values from -6 to 6
- cotangent: bfloat16 [8, 8192, 768], P('dp', 'tm'), may hold values from -6 to 6
- lengths: int32 [8], P('dp'), may hold values from 4096 to 8192, as said below
- rel_bias: float32 [12, 257], replicated, may hold values from -4 to 4
Outputs:
- context: bfloat16 [8, 8192, 768], P('dp', 'tm')
- grad_query: bfloat16 [8, 8192, 768], P('dp', 'tm')
- grad_key: bfloat16 [8, 8192, 768], P('dp', 'tm')
- grad_value: bfloat16 [8, 8192, 768], P('dp', 'tm')
- grad_bias: float32 [12, 257], replicated
Inputs may be any that keep to these rules, and one draw needn't show every extreme that they name: `lengths`: one utterance has all 8192 frames valid and another exactly 4096.
All inputs are finite; a program needn't handle non-finite values.
Results may differ from a plain program's by a relative error of at most 0.005.
Values may be sent and summed in bfloat16 or wider, within the bound.
No kernel may reach another device: no remote copies, remote signals or barrier semaphores. Data moves between devices by JAX's collectives and lax.ppermute only.
A program may use at most 64 MiB of HBM per device.

v0:
```python
import jax
import jax.numpy as jnp
from jax import lax
from jax.sharding import Mesh
from jax.sharding import PartitionSpec as P

H = 12
HD = 64
W = 128
TM = ("tm_0", "tm_1", "tm_2")
DP_TM = ("dp_0", "dp_1", "tm_0", "tm_1", "tm_2")
DP = ("dp_0", "dp_1")
masked_score = -1e30


def padded_2(cells, sides, width):
    for axis, dim in sides:
        count = lax.axis_size(axis)
        ends = count - 1
        head = lax.slice_in_dim(cells, 0, width, axis=dim)
        tail = lax.slice_in_dim(cells, cells.shape[dim] - width, cells.shape[dim], axis=dim)
        cells = jnp.concatenate(
            [
                lax.ppermute(tail, axis, [(i, (i + 1) % count) for i in range(ends)]),
                cells,
                lax.ppermute(head, axis, [((i + 1) % count, i) for i in range(ends)]),
            ],
            axis=dim,
        )
    return cells


def by_axis(x, axes):
    for axis in axes:
        x = lax.psum(x, axis)
    return x


def band_matrix(bias_table, height, breadth):
    num_heads = bias_table.shape[0]
    span_cols = bias_table.shape[1]
    repeated = jnp.broadcast_to(bias_table[:, None, :], (num_heads, height, span_cols))
    padded = jnp.pad(repeated, ((0, 0), (0, 0), (0, breadth + 1 - span_cols)))
    flattened = padded.reshape(num_heads, height * (breadth + 1))[:, : height * breadth]
    return flattened.reshape(num_heads, height, breadth)


def band_sum(values, span_cols):
    num_heads, height, breadth = values.shape
    flattened = jnp.pad(values.reshape(num_heads, height * breadth), ((0, 0), (0, height)))
    return jnp.sum(flattened.reshape(num_heads, height, breadth + 1)[:, :, :span_cols], axis=1)


def heads_first(array, rows):
    return array.reshape(rows, H, HD).transpose(1, 0, 2)


def rows_first(array):
    num_heads, rows, size = array.shape
    return array.transpose(1, 0, 2).reshape(rows, num_heads * size)


def query_side(query_rows, key_rows, value_rows, grad_rows, bias_table, query_pos, key_pos, length):
    scaling = HD ** (-0.5)
    height = query_rows.shape[1]
    breadth = key_rows.shape[1]
    scores = (
        jnp.einsum("hqd,hkd->hqk", query_rows, key_rows, preferred_element_type=jnp.float32)
        * scaling
    )
    scores = scores + band_matrix(bias_table, height, breadth)
    allowed = (
        (jnp.abs(key_pos[None, :] - query_pos[:, None]) <= W)
        & (key_pos[None, :] >= 0)
        & (key_pos[None, :] < length)
    )
    scores = jnp.where(allowed[None], scores, masked_score)
    row_max = jnp.max(scores, axis=-1)
    shifted = jnp.exp(scores - row_max[..., None])
    row_total = jnp.sum(shifted, axis=-1)
    log_total = row_max + jnp.log(row_total)
    attn_probs = shifted / row_total[..., None]
    valid_rows = query_pos < length
    probs_low = attn_probs.astype(jnp.bfloat16)
    mixed = jnp.einsum("hqk,hkd->hqd", probs_low, value_rows, preferred_element_type=jnp.float32)
    context = jnp.where(valid_rows[None, :, None], mixed, 0.0).astype(jnp.bfloat16)
    masked_grad = jnp.where(valid_rows[None, :, None], grad_rows, jnp.zeros_like(grad_rows))
    grad_probs = jnp.einsum(
        "hqd,hkd->hqk", masked_grad, value_rows, preferred_element_type=jnp.float32
    )
    row_delta = jnp.sum(attn_probs * grad_probs, axis=-1)
    grad_scores = attn_probs * (grad_probs - row_delta[..., None])
    grad_low = grad_scores.astype(jnp.bfloat16)
    grad_query = (
        jnp.einsum("hqk,hkd->hqd", grad_low, key_rows, preferred_element_type=jnp.float32) * scaling
    ).astype(jnp.bfloat16)
    grad_table = band_sum(grad_scores, bias_table.shape[1])
    results = (context, grad_query, log_total, row_delta, grad_table)
    return results


def key_side(
    key_rows,
    value_rows,
    query_rows,
    grad_rows,
    log_total,
    row_delta,
    bias_table,
    key_pos,
    query_pos,
    length,
):
    scaling = HD ** (-0.5)
    height = key_rows.shape[1]
    breadth = query_rows.shape[1]
    scores = (
        jnp.einsum("hkd,hqd->hkq", key_rows, query_rows, preferred_element_type=jnp.float32)
        * scaling
    )
    scores = scores + band_matrix(bias_table[:, ::-1], height, breadth)
    valid_query = (query_pos >= 0) & (query_pos < length)
    allowed = (
        (jnp.abs(query_pos[None, :] - key_pos[:, None]) <= W)
        & (key_pos[:, None] < length)
        & valid_query[None, :]
    )
    attn_probs = jnp.where(
        allowed[None], jnp.exp(jnp.where(allowed[None], scores - log_total[:, None, :], 0.0)), 0.0
    )
    probs_low = attn_probs.astype(jnp.bfloat16)
    masked_grad = jnp.where(valid_query[None, :, None], grad_rows, jnp.zeros_like(grad_rows))
    grad_probs = jnp.einsum(
        "hkd,hqd->hkq", value_rows, masked_grad, preferred_element_type=jnp.float32
    )
    grad_scores = attn_probs * (grad_probs - row_delta[:, None, :])
    grad_low = grad_scores.astype(jnp.bfloat16)
    key_grad = (
        jnp.einsum("hkq,hqd->hkd", grad_low, query_rows, preferred_element_type=jnp.float32)
        * scaling
    )
    value_grad = jnp.einsum(
        "hkq,hqd->hkd", probs_low, masked_grad, preferred_element_type=jnp.float32
    )
    return (key_grad, value_grad)


def on_device(query_proj, key_proj, value_proj, cotangent, lengths, rel_bias):
    frames = query_proj.shape[1]
    model_width = query_proj.shape[2]
    extended = frames + 2 * W
    first_frame = lax.axis_index(TM) * frames
    query_pos = first_frame + jnp.arange(frames, dtype=jnp.int32)
    key_pos = first_frame - W + jnp.arange(extended, dtype=jnp.int32)
    length = lengths[0]
    head_group = 4
    groups = H // head_group
    with_rims = padded_2(jnp.stack([key_proj, value_proj, query_proj, cotangent]), ((TM, 2),), W)
    key_ext = heads_first(with_rims[0, 0], extended)
    value_ext = heads_first(with_rims[1, 0], extended)
    query_own = heads_first(query_proj[0], frames)
    grad_own = heads_first(cotangent[0], frames)
    outputs = []
    for group_index in range(groups):
        low_head = group_index * head_group
        high_head = low_head + head_group
        outputs.append(
            query_side(
                query_own[low_head:high_head],
                key_ext[low_head:high_head],
                value_ext[low_head:high_head],
                grad_own[low_head:high_head],
                rel_bias[low_head:high_head],
                query_pos,
                key_pos,
                length,
            )
        )
    context = rows_first(jnp.concatenate([item[0] for item in outputs], axis=0))
    grad_query = rows_first(jnp.concatenate([item[1] for item in outputs], axis=0))
    log_totals = jnp.concatenate([item[2] for item in outputs], axis=0)
    row_deltas = jnp.concatenate([item[3] for item in outputs], axis=0)
    grad_table = jnp.concatenate([item[4] for item in outputs], axis=0)
    row_stats_all = padded_2(jnp.stack([log_totals, row_deltas]), ((TM, 2),), W)
    query_ext = heads_first(with_rims[2, 0], extended)
    grad_ext = heads_first(with_rims[3, 0], extended)
    key_own = heads_first(key_proj[0], frames)
    value_own = heads_first(value_proj[0], frames)
    key_parts = []
    value_parts = []
    for group_index in range(groups):
        low_head = group_index * head_group
        high_head = low_head + head_group
        key_part, value_part = key_side(
            key_own[low_head:high_head],
            value_own[low_head:high_head],
            query_ext[low_head:high_head],
            grad_ext[low_head:high_head],
            row_stats_all[0, low_head:high_head],
            row_stats_all[1, low_head:high_head],
            rel_bias[low_head:high_head],
            query_pos,
            key_pos,
            length,
        )
        key_parts.append(key_part)
        value_parts.append(value_part)
    grad_key = rows_first(jnp.concatenate(key_parts, axis=0)).astype(jnp.bfloat16)
    grad_value = rows_first(jnp.concatenate(value_parts, axis=0)).astype(jnp.bfloat16)
    grad_bias = by_axis(grad_table, DP_TM)
    return (
        context.reshape(1, frames, model_width),
        grad_query.reshape(1, frames, model_width),
        grad_key.reshape(1, frames, model_width),
        grad_value.reshape(1, frames, model_width),
        grad_bias,
    )


def solution(mesh):
    finer = Mesh(mesh.devices.reshape(2, 4, 8, 4, 2), ("dp_0", "dp_1", "tm_0", "tm_1", "tm_2"))
    in_specs = (P(DP, TM, None), P(DP, TM, None), P(DP, TM, None), P(DP, TM, None), P(DP), P())
    out_specs = (P(DP, TM, None), P(DP, TM, None), P(DP, TM, None), P(DP, TM, None), P())
    return jax.shard_map(
        on_device, mesh=finer, in_specs=in_specs, out_specs=out_specs, check_vma=False
    )
```

profile of v0, /device:TPU:1, one launch (start us, length us, event | category | flops | bytes accessed | tf_op | source)
XLA Modules:
  0.0 190.9 jit_solution(16381931620373479713)
XLA Ops:
  3.9 1.2 copy.40
  6.1 8.7 %collective-permute-start.1 = (bf16[4,1,128,768]{2,3,1,0:T(8,128)(2,1)}, bf16[4,1,128,768]{2,3,1,0:T(8,128)(2,1)}, u32[]{:S(2)}, u32[]{:S(2)}) collective-permute-start(bf16[4,1,128,768]{2,3,1,0:T(8,128)(2,1)} %pad_maximum_fusion.1), channel_id=1, source_target_pairs={{1,0},{2,1},{3,2},{4,3},{5,4},{6,5},{7,6},{8,7},{9,8},{10,9},{11,1... | collective-permute-start | bytes 2359304 | tf_op jit(solution)/shard_map/ppermute | solution.py:26
  14.8 1.9 %collective-permute-start = (bf16[4,1,128,768]{2,3,1,0:T(8,128)(2,1)}, bf16[4,1,128,768]{2,3,1,0:T(8,128)(2,1)}, u32[]{:S(2)}, u32[]{:S(2)}) collective-permute-start(bf16[4,1,128,768]{2,3,1,0:T(8,128)(2,1)} %pad_maximum_fusion.1), channel_id=1, source_target_pairs={{0,1},{1,2},{2,3},{3,4},{4,5},{5,6},{6,7},{7,8},{8,9},{9,10},{10,1... | collective-permute-start | bytes 2359304 | tf_op jit(solution)/shard_map/ppermute | solution.py:24
  22.9 1.2 copy.45
  25.8 1.2 copy.67
  28.7 1.2 copy.65
  33.6 1.6 pad_maximum_fusion
  35.2 1.3 fusion.128
  39.7 1.2 multiply_reduce_fusion.1
  42.3 1.2 multiply_reduce_fusion.2
  44.2 3.3 %collective-permute-start.3 = (f32[2,12,128]{2,1,0:T(8,128)}, f32[2,12,128]{2,1,0:T(8,128)}, u32[]{:S(2)}, u32[]{:S(2)}) collective-permute-start(f32[2,12,128]{2,1,0:T(8,128)} %pad_maximum_fusion.7), channel_id=1, source_target_pairs={{1,0},{2,1},{3,2},{4,3},{5,4},{6,5},{7,6},{8,7},{9,8},{10,9},{11,1... | collective-permute-start | bytes 36872 | tf_op jit(solution)/shard_map/ppermute | solution.py:26
  47.5 2.4 %collective-permute-start.2 = (f32[2,12,128]{2,1,0:T(8,128)}, f32[2,12,128]{2,1,0:T(8,128)}, u32[]{:S(2)}, u32[]{:S(2)}) collective-permute-start(f32[2,12,128]{2,1,0:T(8,128)} %pad_maximum_fusion.7), channel_id=1, source_target_pairs={{0,1},{1,2},{2,3},{3,4},{4,5},{5,6},{6,7},{7,8},{8,9},{9,10},{10,1... | collective-permute-start | bytes 36872 | tf_op jit(solution)/shard_map/ppermute | solution.py:24
  50.3 1.1 copy.74
  51.5 1.3 subtract_multiply_fusion.1
  53.0 1.1 copy.73
  54.1 1.3 subtract_multiply_fusion.2
  63.1 23.4 %psum.35 = f32[12,257]{1,0:T(8,128)S(1)} all-reduce(f32[12,257]{1,0:T(8,128)S(1)} %pad_maximum_fusion.6), channel_id=1, replica_groups=mesh['dp_0'=2,'dp_1'=4,'tm_0'=8,'tm_1'=4,'tm_2'=2] {'dp_0'}, use_global_device_ids=true, to_apply=%region_12.13 | all-reduce | flops 3084 | bytes 24672 | tf_op jit(solution)/shard_map/psum | solution.py:35
  86.5 13.5 %psum.36 = f32[12,257]{1,0:T(8,128)S(1)} all-reduce(f32[12,257]{1,0:T(8,128)S(1)} %psum.35), channel_id=1, replica_groups=mesh['dp_0'=2,'dp_1'=4,'tm_0'=8,'tm_1'=4,'tm_2'=2] {'dp_1'}, use_global_device_ids=true, to_apply=%region_13.14 | all-reduce | flops 3084 | bytes 24672 | tf_op jit(solution)/shard_map/psum | solution.py:35
  100.0 45.1 %psum.37 = f32[12,257]{1,0:T(8,128)S(1)} all-reduce(f32[12,257]{1,0:T(8,128)S(1)} %psum.36), channel_id=1, replica_groups=mesh['dp_0'=2,'dp_1'=4,'tm_0'=8,'tm_1'=4,'tm_2'=2] {'tm_0'}, use_global_device_ids=true, to_apply=%region_14.15 | all-reduce | flops 3084 | bytes 24672 | tf_op jit(solution)/shard_map/psum | solution.py:35
  145.1 15.4 %psum.38 = f32[12,257]{1,0:T(8,128)S(1)} all-reduce(f32[12,257]{1,0:T(8,128)S(1)} %psum.37), channel_id=1, replica_groups=mesh['dp_0'=2,'dp_1'=4,'tm_0'=8,'tm_1'=4,'tm_2'=2] {'tm_1'}, use_global_device_ids=true, to_apply=%region_15.16 | all-reduce | flops 3084 | bytes 24672 | tf_op jit(solution)/shard_map/psum | solution.py:35
  160.5 19.3 %psum.39 = f32[12,257]{1,0:T(8,128)} all-reduce(f32[12,257]{1,0:T(8,128)S(1)} %psum.38), channel_id=1, replica_groups=mesh['dp_0'=2,'dp_1'=4,'tm_0'=8,'tm_1'=4,'tm_2'=2] {'tm_2'}, use_global_device_ids=true, to_apply=%region_16.17 | all-reduce | flops 3084 | bytes 24672 | tf_op jit(solution)/shard_map/psum | solution.py:35
  180.6 1.6 fusion.5
  184.6 1.7 fusion.35
  186.3 1.7 fusion.34
  (145 shorter events, 35.9 us)
Async XLA Ops:
  0.6 16.1 %copy-start.20 = (f32[12,257]{1,0:T(8,128)S(1)}, f32[12,257]{1,0:T(8,128)}, u32[]{:S(2)}) copy-start(f32[12,257]{1,0:T(8,128)} %param.11) | copy-start | bytes 37012
  3.9 29.7 %copy-start.5 = (bf16[1,128,768]{1,2,0:T(8,128)(2,1)}, bf16[1,128,768]{1,2,0:T(8,128)(2,1)S(1)}, u32[]{:S(2)}) copy-start(bf16[1,128,768]{1,2,0:T(8,128)(2,1)S(1)} %copy.41) | copy-start | bytes 589828
  5.1 28.5 %copy-start.7 = (bf16[1,128,768]{1,2,0:T(8,128)(2,1)}, bf16[1,128,768]{1,2,0:T(8,128)(2,1)S(1)}, u32[]{:S(2)}) copy-start(bf16[1,128,768]{1,2,0:T(8,128)(2,1)S(1)} %copy.40) | copy-start | bytes 589828
  6.1 27.5 %collective-permute-start.1 = (bf16[4,1,128,768]{2,3,1,0:T(8,128)(2,1)}, bf16[4,1,128,768]{2,3,1,0:T(8,128)(2,1)}, u32[]{:S(2)}, u32[]{:S(2)}) collective-permute-start(bf16[4,1,128,768]{2,3,1,0:T(8,128)(2,1)} %pad_maximum_fusion.1), channel_id=1, source_target_pairs={{1,0},{2,1},{3,2},{4,3},{5,4},{6,5},{7,6},{8,7},{9,8},{10,9},{11,1... | collective-permute-start | bytes 2359304 | tf_op jit(solution)/shard_map/ppermute | solution.py:26
  14.8 18.8 %collective-permute-start = (bf16[4,1,128,768]{2,3,1,0:T(8,128)(2,1)}, bf16[4,1,128,768]{2,3,1,0:T(8,128)(2,1)}, u32[]{:S(2)}, u32[]{:S(2)}) collective-permute-start(bf16[4,1,128,768]{2,3,1,0:T(8,128)(2,1)} %pad_maximum_fusion.1), channel_id=1, source_target_pairs={{0,1},{1,2},{2,3},{3,4},{4,5},{5,6},{6,7},{7,8},{8,9},{9,10},{10,1... | collective-permute-start | bytes 2359304 | tf_op jit(solution)/shard_map/ppermute | solution.py:24
  35.2 1.7 copy-start.1
  39.7 1.2 copy-start
  43.6 6.4 %copy-start.14 = (f32[1,12,128]{2,1,0:T(8,128)}, f32[1,12,128]{2,1,0:T(8,128)S(1)}, u32[]{:S(2)}) copy-start(f32[1,12,128]{2,1,0:T(8,128)S(1)} %maximum_bitcast_fusion) | copy-start | bytes 18436
  44.2 135.6 %collective-permute-start.3 = (f32[2,12,128]{2,1,0:T(8,128)}, f32[2,12,128]{2,1,0:T(8,128)}, u32[]{:S(2)}, u32[]{:S(2)}) collective-permute-start(f32[2,12,128]{2,1,0:T(8,128)} %pad_maximum_fusion.7), channel_id=1, source_target_pairs={{1,0},{2,1},{3,2},{4,3},{5,4},{6,5},{7,6},{8,7},{9,8},{10,9},{11,1... | collective-permute-start | bytes 36872 | tf_op jit(solution)/shard_map/ppermute | solution.py:26
  47.5 132.3 %collective-permute-start.2 = (f32[2,12,128]{2,1,0:T(8,128)}, f32[2,12,128]{2,1,0:T(8,128)}, u32[]{:S(2)}, u32[]{:S(2)}) collective-permute-start(f32[2,12,128]{2,1,0:T(8,128)} %pad_maximum_fusion.7), channel_id=1, source_target_pairs={{0,1},{1,2},{2,3},{3,4},{4,5},{5,6},{6,7},{7,8},{8,9},{9,10},{10,1... | collective-permute-start | bytes 36872 | tf_op jit(solution)/shard_map/ppermute | solution.py:24
  54.1 1.9 copy-start.16
  54.1 1.9 copy-start.17
  54.1 1.9 copy-start.18
  55.5 2.2 %copy-start.2 = (f32[4,128,384]{2,1,0:T(8,128)S(1)}, f32[4,128,384]{2,1,0:T(8,128)}, u32[]{:S(2)}) copy-start(f32[4,128,384]{2,1,0:T(8,128)} %copy.74) | copy-start | bytes 2359300
  58.2 1.3 copy-start.3
  61.8 118.0 %copy-start.15 = (f32[1,12,128]{2,1,0:T(8,128)S(1)}, f32[1,12,128]{2,1,0:T(8,128)}, u32[]{:S(2)}) copy-start(f32[1,12,128]{2,1,0:T(8,128)} %copy-done.14) | copy-start | bytes 18436
  61.8 118.8 %copy-start.8 = (bf16[1,128,768]{1,2,0:T(8,128)(2,1)S(1)}, bf16[1,128,768]{1,2,0:T(8,128)(2,1)}, u32[]{:S(2)}) copy-start(bf16[1,128,768]{1,2,0:T(8,128)(2,1)} %copy-done.7) | copy-start | bytes 589828
  61.8 118.8 %copy-start.13 = (bf16[1,1,384,768]{2,3,1,0:T(8,128)(2,1)S(1)}, bf16[1,1,384,768]{2,3,1,0:T(8,128)(2,1)}, u32[]{:S(2)}) copy-start(bf16[1,1,384,768]{2,3,1,0:T(8,128)(2,1)} %get-tuple-element.18) | copy-start | bytes 1769476
  61.8 118.8 %copy-start.19 = (pred[128,384]{0,1:T(8,128)(4,1)S(1)}, pred[128,384]{0,1:T(8,128)(4,1)}, u32[]{:S(2)}) copy-start(pred[128,384]{0,1:T(8,128)(4,1)} %get-tuple-element.30) | copy-start | bytes 147460
  62.0 120.3 %copy-start.10 = (f32[4,128,384]{1,2,0:T(8,128)S(1)}, f32[4,128,384]{1,2,0:T(8,128)}, u32[]{:S(2)}) copy-start(f32[4,128,384]{1,2,0:T(8,128)} %copy.65) | copy-start | bytes 2359300
  180.6 2.2 %copy-start.4 = (bf16[1,1,384,768]{2,3,1,0:T(8,128)(2,1)S(1)}, bf16[1,1,384,768]{2,3,1,0:T(8,128)(2,1)}, u32[]{:S(2)}) copy-start(bf16[1,1,384,768]{2,3,1,0:T(8,128)(2,1)} %get-tuple-element.17) | copy-start | bytes 1769476
  182.3 1.6 copy-start.12
  182.3 2.3 %copy-start.6 = (bf16[1,128,768]{1,2,0:T(8,128)(2,1)S(1)}, bf16[1,128,768]{1,2,0:T(8,128)(2,1)}, u32[]{:S(2)}) copy-start(bf16[1,128,768]{1,2,0:T(8,128)(2,1)} %copy-done.5) | copy-start | bytes 589828
  182.8 5.2 %copy-start.9 = (f32[4,128,384]{1,2,0:T(8,128)S(1)}, f32[4,128,384]{1,2,0:T(8,128)}, u32[]{:S(2)}) copy-start(f32[4,128,384]{1,2,0:T(8,128)} %copy.62) | copy-start | bytes 2359300
  (1 other events, 0.9 us)
where the time goes:
time: 192 us; the launch traced here: 191 us
  blocking collectives  117 us (61%)
  local copies, waits for them, and re-layouts  32.3 us (17%)
  starting transfers between devices  16.4 us (9%)
  matrix products  14.2 us (7%)
  other arithmetic  9.12 us (5%)
  between operations  2.11 us (1%)
    psum x5, blocking collectives, by_axis(): x = lax.psum(x, axis)  117 us
    ppermute x2, starting transfers between devices, padded_2(): lax.ppermute(head, axis, [((i + 1) % count, i) for i in range(ends)])  12 us
    unnamed x65, local copies, waits for them, and re-layouts  11.4 us
    reshape x6, local copies, waits for them, and re-layouts, band_matrix(): padded.reshape(num_heads, height * (breadth + 1))[:, :height * breadth]  6.24 us
    reshape x6, local copies, waits for them, and re-layouts, band_matrix(): return flattened.reshape(num_heads, height, breadth)  6.05 us
    ppermute x2, starting transfers between devices, padded_2(): lax.ppermute(tail, axis, [(i, (i + 1) % count) for i in range(ends)])  4.34 us
    dot_general x3, matrix products, key_side(): jnp.einsum('hkq,hqd->hkd', grad_low, query_rows, preferred_element_type=j...  3.87 us
  transfers between devices with their start and end apart: 4, of which 0 were waited for; matrix products, arithmetic and copies ran while one was open for 15% of the time, Pallas kernels for 0%

commit v1 on v0

--- a/solution.py
+++ b/solution.py
@@ -32,7 +32,8 @@
 
 def by_axis(x, axes):
     for axis in axes:
-        x = lax.psum(x, axis)
+        parts = lax.all_gather(x, axis)
+        x = jnp.sum(parts, axis=0)
     return x
 
 

time: 192 us -> 163 us (0.85)
  blocking collectives: 117 us -> 87.1 us
    psum x5 -> x0, blocking collectives: 117 us -> none  [by_axis(): x = lax.psum(x, axis)]
    all_gather x0 -> x5, blocking collectives: none -> 87.1 us  [by_axis(): parts = lax.all_gather(x, axis)]
    unnamed x65 -> x67, local copies, waits for them, and re-layouts: 11.4 us -> 10.7 us
  transfers between devices with their start and end apart: 4 -> 4, of which waited for: 0 -> 0; matrix products, arithmetic and copies ran while one was open for 15% -> 19% of each run, Pallas kernels for 0% -> 0%
where the time goes in v1:
time: 163 us
  blocking collectives  87.1 us (53%)
  local copies, waits for them, and re-layouts  32.6 us (20%)
  starting transfers between devices  16.4 us (10%)
  matrix products  14.1 us (9%)
  other arithmetic  10.4 us (6%)
  between operations  2.12 us (1%)
    all_gather x5, blocking collectives, by_axis(): parts = lax.all_gather(x, axis)  87.1 us
    ppermute x2, starting transfers between devices, padded_2(): lax.ppermute(head, axis, [((i + 1) % count, i) for i in range(ends)])  12 us
    unnamed x67, local copies, waits for them, and re-layouts  10.7 us
    reshape x6, local copies, waits for them, and re-layouts, band_matrix(): padded.reshape(num_heads, height * (breadth + 1))[:, :height * breadth]  6.24 us
    reshape x6, local copies, waits for them, and re-layouts, band_matrix(): return flattened.reshape(num_heads, height, breadth)  6.05 us
    ppermute x2, starting transfers between devices, padded_2(): lax.ppermute(tail, axis, [(i, (i + 1) % count) for i in range(ends)])  4.34 us
    dot_general x3, matrix products, key_side(): jnp.einsum('hkd,hqd->hkq', key_rows, query_rows, preferred_element_type=j...  3.56 us
    mul x3, local copies, waits for them, and re-layouts, query_side(): grad_scores = attn_probs * (grad_probs - row_delta[..., None])  3.47 us
  transfers between devices with their start and end apart: 4, of which 0 were waited for; matrix products, arithmetic and copies ran while one was open for 19% of the time, Pallas kernels for 0%

profile of v1, /device:TPU:1, one launch (start us, length us, event | category | flops | bytes accessed | tf_op | source)
XLA Modules:
  0.0 162.8 jit_solution(11179882690738038685)
XLA Ops:
  1.8 1.2 copy.81
  6.1 8.7 %collective-permute-start.1 = (bf16[4,1,128,768]{2,3,1,0:T(8,128)(2,1)}, bf16[4,1,128,768]{2,3,1,0:T(8,128)(2,1)}, u32[]{:S(2)}, u32[]{:S(2)}) collective-permute-start(bf16[4,1,128,768]{2,3,1,0:T(8,128)(2,1)} %pad_maximum_fusion.1), channel_id=1, source_target_pairs={{1,0},{2,1},{3,2},{4,3},{5,4},{6,5},{7,6},{8,7},{9,8},{10,9},{11,1... | collective-permute-start | bytes 2359304 | tf_op jit(solution)/shard_map/ppermute | solution.py:26
  14.8 1.9 %collective-permute-start = (bf16[4,1,128,768]{2,3,1,0:T(8,128)(2,1)}, bf16[4,1,128,768]{2,3,1,0:T(8,128)(2,1)}, u32[]{:S(2)}, u32[]{:S(2)}) collective-permute-start(bf16[4,1,128,768]{2,3,1,0:T(8,128)(2,1)} %pad_maximum_fusion.1), channel_id=1, source_target_pairs={{0,1},{1,2},{2,3},{3,4},{4,5},{5,6},{6,7},{7,8},{8,9},{9,10},{10,1... | collective-permute-start | bytes 2359304 | tf_op jit(solution)/shard_map/ppermute | solution.py:24
  22.9 1.2 copy.84
  25.8 1.2 copy.106
  28.7 1.2 copy.104
  33.7 1.6 pad_maximum_fusion
  35.2 1.3 fusion.128
  39.7 1.2 multiply_reduce_fusion.1
  42.3 1.2 multiply_reduce_fusion.2
  44.2 3.3 %collective-permute-start.3 = (f32[2,12,128]{2,1,0:T(8,128)}, f32[2,12,128]{2,1,0:T(8,128)}, u32[]{:S(2)}, u32[]{:S(2)}) collective-permute-start(f32[2,12,128]{2,1,0:T(8,128)} %pad_maximum_fusion.6), channel_id=1, source_target_pairs={{1,0},{2,1},{3,2},{4,3},{5,4},{6,5},{7,6},{8,7},{9,8},{10,9},{11,1... | collective-permute-start | bytes 36872 | tf_op jit(solution)/shard_map/ppermute | solution.py:26
  47.5 2.4 %collective-permute-start.2 = (f32[2,12,128]{2,1,0:T(8,128)}, f32[2,12,128]{2,1,0:T(8,128)}, u32[]{:S(2)}, u32[]{:S(2)}) collective-permute-start(f32[2,12,128]{2,1,0:T(8,128)} %pad_maximum_fusion.6), channel_id=1, source_target_pairs={{0,1},{1,2},{2,3},{3,4},{4,5},{5,6},{6,7},{7,8},{8,9},{9,10},{10,1... | collective-permute-start | bytes 36872 | tf_op jit(solution)/shard_map/ppermute | solution.py:24
  51.5 1.3 subtract_multiply_fusion.1
  54.2 1.4 subtract_multiply_fusion.2
  55.8 1.2 copy.111
  62.3 12.1 %all-gather.5 = f32[2,12,257]{2,1,0:T(8,128)S(1)} all-gather(f32[1,12,257]{2,1,0:T(8,128)S(1)} %maximum_bitcast_fusion), channel_id=2, replica_groups=mesh['dp_0'=2,'dp_1'=4,'tm_0'=8,'tm_1'=4,'tm_2'=2] {'dp_0'}, dimensions={0}, use_global_device_ids=true | all-gather | bytes 37008 | tf_op jit(solution)/shard_map/all_gather | solution.py:35
  74.4 9.2 %all-gather.6 = f32[4,12,257]{2,1,0:T(8,128)S(1)} all-gather(f32[1,12,257]{2,1,0:T(8,128)S(1)} %bitcast.241), channel_id=3, replica_groups=mesh['dp_0'=2,'dp_1'=4,'tm_0'=8,'tm_1'=4,'tm_2'=2] {'dp_1'}, dimensions={0}, use_global_device_ids=true | all-gather | bytes 61680 | tf_op jit(solution)/shard_map/all_gather | solution.py:35
  83.6 40.1 %all-gather.7 = f32[8,12,257]{2,1,0:T(8,128)S(1)} all-gather(f32[1,12,257]{2,1,0:T(8,128)S(1)} %bitcast.240), channel_id=4, replica_groups=mesh['dp_0'=2,'dp_1'=4,'tm_0'=8,'tm_1'=4,'tm_2'=2] {'tm_0'}, dimensions={0}, use_global_device_ids=true | all-gather | bytes 111024 | tf_op jit(solution)/shard_map/all_gather | solution.py:35
  123.8 13.5 %all-gather.8 = f32[4,12,257]{2,1,0:T(8,128)S(1)} all-gather(f32[1,12,257]{2,1,0:T(8,128)S(1)} %bitcast.239), channel_id=5, replica_groups=mesh['dp_0'=2,'dp_1'=4,'tm_0'=8,'tm_1'=4,'tm_2'=2] {'tm_1'}, dimensions={0}, use_global_device_ids=true | all-gather | bytes 61680 | tf_op jit(solution)/shard_map/all_gather | solution.py:35
  139.0 12.2 %all-gather.9 = f32[2,12,257]{2,1,0:T(8,128)S(1)} all-gather(f32[1,12,257]{2,1,0:T(8,128)S(1)} %bitcast.242), channel_id=6, replica_groups=mesh['dp_0'=2,'dp_1'=4,'tm_0'=8,'tm_1'=4,'tm_2'=2] {'tm_2'}, dimensions={0}, use_global_device_ids=true | all-gather | bytes 37008 | tf_op jit(solution)/shard_map/all_gather | solution.py:35
  151.9 1.4 maximum_bitcast_fusion.6
  153.2 1.4 fusion.5
  154.7 1.7 %fusion.11 = f32[4,128,384]{1,2,0:T(8,128)S(1)} fusion(f32[4,128,384]{1,2,0:T(8,128)S(1)} %copy-done.10, bf16[12,384,64]{1,2,0:T(8,128)(2,1)} %bitcast.228, f32[4,384]{1,0:T(4,128)S(1)} %get-tuple-element.29, pred[128,384]{0,1:T(8,128)(4,1)} %get-tuple-element.35, bf16[12,128,64]{1,2,0:T(8,128)(2,1)S(1)} %bitcast.216), kind=kOutput, calls=%fused_computation.14 | convolution fusion | flops 26148864 | bytes 2283520 | tf_op jit(solution)/shard_map/hkd,hqd->hkq/dot_general | solution.py:119
  157.6 1.7 %fusion.35 = bf16[4,128,64]{1,2,0:T(8,128)(2,1)S(1)} fusion(f32[4,128,384]{1,2,0:T(8,128)} %copy-done.11, f32[4,384]{1,0:T(4,128)S(1)} %get-tuple-element.31, bf16[12,384,64]{1,2,0:T(8,128)(2,1)S(1)} %bitcast.229, bf16[12,384,64]{1,2,0:T(8,128)(2,1)S(1)} %bitcast.204, pred[384]{0:T(512)(128)(4,1)S(1)} %copy-done.19, bf16[12,128,64]{1,2,0:T(8,128)(2,1)S(1)} %bitcast.210), kind=kOutput, calls=%fused_computation.51 | convolution fusion | flops 51085312 | bytes 1317376 | tf_op jit(solution)/shard_map/hkq,hqd->hkd/dot_general | solution.py:140
  (152 shorter events, 37.3 us)
Async XLA Ops:
  0.6 16.1 %copy-start.17 = (f32[12,257]{1,0:T(8,128)S(1)}, f32[12,257]{1,0:T(8,128)}, u32[]{:S(2)}) copy-start(f32[12,257]{1,0:T(8,128)} %param.11) | copy-start | bytes 37012
  1.7 31.9 %copy-start.6 = (bf16[1,128,768]{1,2,0:T(8,128)(2,1)}, bf16[1,128,768]{1,2,0:T(8,128)(2,1)S(1)}, u32[]{:S(2)}) copy-start(bf16[1,128,768]{1,2,0:T(8,128)(2,1)S(1)} %copy.82) | copy-start | bytes 589828
  6.1 27.5 %collective-permute-start.1 = (bf16[4,1,128,768]{2,3,1,0:T(8,128)(2,1)}, bf16[4,1,128,768]{2,3,1,0:T(8,128)(2,1)}, u32[]{:S(2)}, u32[]{:S(2)}) collective-permute-start(bf16[4,1,128,768]{2,3,1,0:T(8,128)(2,1)} %pad_maximum_fusion.1), channel_id=1, source_target_pairs={{1,0},{2,1},{3,2},{4,3},{5,4},{6,5},{7,6},{8,7},{9,8},{10,9},{11,1... | collective-permute-start | bytes 2359304 | tf_op jit(solution)/shard_map/ppermute | solution.py:26
  14.8 18.8 %collective-permute-start = (bf16[4,1,128,768]{2,3,1,0:T(8,128)(2,1)}, bf16[4,1,128,768]{2,3,1,0:T(8,128)(2,1)}, u32[]{:S(2)}, u32[]{:S(2)}) collective-permute-start(bf16[4,1,128,768]{2,3,1,0:T(8,128)(2,1)} %pad_maximum_fusion.1), channel_id=1, source_target_pairs={{0,1},{1,2},{2,3},{3,4},{4,5},{5,6},{6,7},{7,8},{8,9},{9,10},{10,1... | collective-permute-start | bytes 2359304 | tf_op jit(solution)/shard_map/ppermute | solution.py:24
  35.2 1.7 %copy-start.1 = (f32[4,128,384]{1,2,0:T(8,128)S(1)}, f32[4,128,384]{1,2,0:T(8,128)}, u32[]{:S(2)}) copy-start(f32[4,128,384]{1,2,0:T(8,128)} %copy.86) | copy-start | bytes 2359300
  39.7 1.2 copy-start
  44.2 107.6 %collective-permute-start.3 = (f32[2,12,128]{2,1,0:T(8,128)}, f32[2,12,128]{2,1,0:T(8,128)}, u32[]{:S(2)}, u32[]{:S(2)}) collective-permute-start(f32[2,12,128]{2,1,0:T(8,128)} %pad_maximum_fusion.6), channel_id=1, source_target_pairs={{1,0},{2,1},{3,2},{4,3},{5,4},{6,5},{7,6},{8,7},{9,8},{10,9},{11,1... | collective-permute-start | bytes 36872 | tf_op jit(solution)/shard_map/ppermute | solution.py:26
  47.5 104.3 %collective-permute-start.2 = (f32[2,12,128]{2,1,0:T(8,128)}, f32[2,12,128]{2,1,0:T(8,128)}, u32[]{:S(2)}, u32[]{:S(2)}) collective-permute-start(f32[2,12,128]{2,1,0:T(8,128)} %pad_maximum_fusion.6), channel_id=1, source_target_pairs={{0,1},{1,2},{2,3},{3,4},{4,5},{5,6},{6,7},{7,8},{8,9},{9,10},{10,1... | collective-permute-start | bytes 36872 | tf_op jit(solution)/shard_map/ppermute | solution.py:24
  54.2 2.8 %copy-start.2 = (f32[4,128,384]{2,1,0:T(8,128)S(1)}, f32[4,128,384]{2,1,0:T(8,128)}, u32[]{:S(2)}) copy-start(f32[4,128,384]{2,1,0:T(8,128)} %copy.113) | copy-start | bytes 2359300
  57.4 1.3 copy-start.3
  59.2 1.3 copy-start.4
  61.0 62.7 %copy-start.13 = (bf16[4,128,64]{1,2,0:T(8,128)(2,1)S(1)}, bf16[4,128,64]{1,2,0:T(8,128)(2,1)}, u32[]{:S(2)}) copy-start(bf16[4,128,64]{1,2,0:T(8,128)(2,1)} %fusion.29) | copy-start | bytes 196612
  61.0 62.7 %copy-start.14 = (bf16[4,128,64]{1,2,0:T(8,128)(2,1)S(1)}, bf16[4,128,64]{1,2,0:T(8,128)(2,1)}, u32[]{:S(2)}) copy-start(bf16[4,128,64]{1,2,0:T(8,128)(2,1)} %fusion.28) | copy-start | bytes 196612
  61.0 62.7 %copy-start.15 = (bf16[4,128,64]{1,2,0:T(8,128)(2,1)S(1)}, bf16[4,128,64]{1,2,0:T(8,128)(2,1)}, u32[]{:S(2)}) copy-start(bf16[4,128,64]{1,2,0:T(8,128)(2,1)} %fusion.27) | copy-start | bytes 196612
  61.2 92.0 %copy-start.8 = (f32[4,128,384]{1,2,0:T(8,128)S(1)}, f32[4,128,384]{1,2,0:T(8,128)}, u32[]{:S(2)}) copy-start(f32[4,128,384]{1,2,0:T(8,128)} %copy.106) | copy-start | bytes 2359300
  123.7 31.0 %copy-start.10 = (f32[4,128,384]{1,2,0:T(8,128)S(1)}, f32[4,128,384]{1,2,0:T(8,128)}, u32[]{:S(2)}) copy-start(f32[4,128,384]{1,2,0:T(8,128)} %copy.104) | copy-start | bytes 2359300
  153.2 3.2 %copy-start.5 = (bf16[1,1,384,768]{2,3,1,0:T(8,128)(2,1)S(1)}, bf16[1,1,384,768]{2,3,1,0:T(8,128)(2,1)}, u32[]{:S(2)}) copy-start(bf16[1,1,384,768]{2,3,1,0:T(8,128)(2,1)} %get-tuple-element.22) | copy-start | bytes 1769476
  153.2 3.2 %copy-start.19 = (pred[384]{0:T(512)(128)(4,1)S(1)}, pred[384]{0:T(512)(128)(4,1)}, u32[]{:S(2)}) copy-start(pred[384]{0:T(512)(128)(4,1)} %copy-done.18) | copy-start | bytes 1156
  154.7 1.7 %copy-start.11 = (f32[4,128,384]{1,2,0:T(8,128)}, f32[4,128,384]{1,2,0:T(8,128)S(1)}, u32[]{:S(2)}) copy-start(f32[4,128,384]{1,2,0:T(8,128)S(1)} %fusion.5) | copy-start | bytes 2359300
  154.7 2.9 %copy-start.12 = (bf16[1,1,384,768]{2,3,1,0:T(8,128)(2,1)S(1)}, bf16[1,1,384,768]{2,3,1,0:T(8,128)(2,1)}, u32[]{:S(2)}) copy-start(bf16[1,1,384,768]{2,3,1,0:T(8,128)(2,1)} %get-tuple-element.23) | copy-start | bytes 1769476
  156.4 3.4 %copy-start.9 = (f32[4,128,384]{1,2,0:T(8,128)S(1)}, f32[4,128,384]{1,2,0:T(8,128)}, u32[]{:S(2)}) copy-start(f32[4,128,384]{1,2,0:T(8,128)} %copy.101) | copy-start | bytes 2359300
  156.4 3.4 %copy-start.16 = (pred[128,384]{0,1:T(8,128)(4,1)S(1)}, pred[128,384]{0,1:T(8,128)(4,1)}, u32[]{:S(2)}) copy-start(pred[128,384]{0,1:T(8,128)(4,1)} %get-tuple-element.35) | copy-start | bytes 147460
  159.3 1.3 copy-start.20
  159.3 1.3 copy-start.21
  (2 other events, 2.0 us)
